TPU v7x, 256 devices: a whole 4x4x8 slice. The times are simulated.
256 devices in a mesh: dp: 2 (over core), expert: 128 (over z, x, y).
Axes of the slice: x: 4, y: 4, z: 8, core: 2. Of those that a mesh axis runs over, the one named last changes fastest.
Arguments:
- tokens: bfloat16 [32768, 2048], P(('dp', 'expert')), may hold values from -6 to 6
- out_grad: bfloat16 [32768, 2048], P(('dp', 'expert')), may hold values from -6 to 6
- expert_ids: int32 [32768, 4], P(('dp', 'expert')), may hold values from 0 to 127, as said below
- gate_weights: float32 [32768, 4], P(('dp', 'expert')), may hold values from 0.05 to 0.6
- w_in: bfloat16 [128, 2048, 768], P('expert'), may hold values from -0.125 to 0.125
- w_out: bfloat16 [128, 384, 2048], P('expert'), may hold values from -0.3125 to 0.3125
Outputs:
- token_grad: bfloat16 [32768, 2048], P(('dp', 'expert'))
- w_in_grad: bfloat16 [128, 2048, 768], P('expert', 'dp')
- w_out_grad: bfloat16 [128, 384, 2048], P('expert', None, 'dp')
Inputs may be any that keep to these rules, and one draw needn't show every extreme that they name: `expert_ids`: each token names 4 different experts; among the 128 tokens of one device no expert is named more than 7 times, and in every device's tokens some expert is named exactly 7 times.
All inputs are finite; a program needn't handle non-finite values.
Results may differ from a plain program's by a relative error of at most 0.0065.
Values may be sent and summed in bfloat16 or wider, within the bound.
No kernel may reach another device: no remote copies, remote signals or barrier semaphores. Data moves between devices by JAX's collectives and lax.ppermute only.
A program may use at most 128 MiB of HBM per device.

v0:
```python
import jax
import jax.numpy as jnp
from jax import lax
from jax.sharding import Mesh
from jax.sharding import PartitionSpec as P

Z, X, Y = (8, 4, 4)
PLANE = X * Y
CAP = 7
IN_CHUNKS = 1
GRAD_CHUNKS = 1
BACK_CHUNKS = 1
f32 = jnp.float32
bf16 = jnp.bfloat16


def mm(a, b, ca, cb):
    return lax.dot_general(a, b, (((ca,), (cb,)), ((), ())), preferred_element_type=f32)


def pieces(width, count):
    step = width // count
    return [(i * step, (i + 1) * step) for i in range(count)]


def silu_parts(gate_part):
    sigma = 1.0 / (1.0 + jnp.exp(-gate_part))
    return (gate_part * sigma, sigma * (1.0 + gate_part * (1.0 - sigma)))


def routing(meta, plane):
    sources, tok = (Z, meta.shape[-1])
    meta = meta.reshape(sources, 8, tok)
    ids = meta[:, :4].astype(jnp.int32)
    gates = meta[:, 4:]
    local = plane * PLANE + jnp.arange(PLANE, dtype=jnp.int32)
    match = ids[:, :, None, :] == local[None, None, :, None]
    named = jnp.any(match, axis=1)
    gate = jnp.sum(jnp.where(match, gates[:, :, None, :], 0.0), axis=1)
    index = jnp.arange(tok, dtype=jnp.int32)
    earlier = (index[:, None] < index[None, :]).astype(bf16)
    before = mm(named.astype(bf16).reshape(sources * PLANE, tok), earlier, 1, 0)
    rank = jnp.where(named, before.reshape(sources, PLANE, tok), -1.0)
    rank = rank.transpose(1, 0, 2)
    gate = gate.transpose(1, 0, 2)
    slot_rank = jnp.arange(CAP, dtype=jnp.int32).astype(f32)
    hit = rank[:, None] == slot_rank[None, :, None, None]
    slot_gate = jnp.sum(jnp.where(hit, gate[:, None], 0.0), axis=3).reshape(-1, 1)
    same = jnp.arange(sources)[:, None] == jnp.arange(sources)[None, :]
    wide = jnp.where(same[None, :, :, None], rank[:, None], -1.0).reshape(
        PLANE, 1, sources, sources * tok
    )
    slots = (wide == slot_rank[None, :, None, None]).astype(bf16)
    return (slots.reshape(PLANE * CAP * sources, sources * tok), slot_gate)


def body(tokens, out_grad, expert_ids, gate_weights, w_in, w_out):
    width = tokens.shape[1]
    w_in, w_out = (w_in[0], w_out[0])
    half = w_out.shape[0]
    plane = lax.axis_index("z")
    core = lax.axis_index("dp")

    def gather_z(x):
        return lax.all_gather(x, "z", axis=0, tiled=True)

    def swap_plane(x):
        return lax.all_to_all(x, ("x", "y"), split_axis=0, concat_axis=0, tiled=True)

    meta = gather_z(jnp.concatenate([expert_ids.astype(f32), gate_weights], axis=1).T)
    slots, slot_gate = routing(meta, plane)
    rows_in = []
    for lo, hi in pieces(width, IN_CHUNKS):
        every = gather_z(tokens[:, lo:hi])
        rows_in.append(swap_plane(mm(slots, every, 1, 0).astype(bf16)))
    rows_grad = []
    for lo, hi in pieces(width, GRAD_CHUNKS):
        every = gather_z(out_grad[:, lo:hi])
        rows_grad.append(swap_plane((mm(slots, every, 1, 0) * slot_gate).astype(bf16)))
    joined = sum(
        (mm(r, w_in[lo:hi], 1, 0) for r, (lo, hi) in zip(rows_in, pieces(width, IN_CHUNKS)))
    )
    d_hidden = sum(
        (mm(r, w_out[:, lo:hi], 1, 1) for r, (lo, hi) in zip(rows_grad, pieces(width, GRAD_CHUNKS)))
    )
    gate_part, up_part = (joined[:, :half], joined[:, half:])
    activated, derivative = silu_parts(gate_part)
    hidden = (activated * up_part).astype(bf16)
    d_joined = jnp.concatenate(
        [d_hidden * up_part * derivative, d_hidden * activated], axis=1
    ).astype(bf16)
    token_grad = []
    for lo, hi in pieces(width, BACK_CHUNKS):
        back = swap_plane(mm(d_joined, w_in[lo:hi], 1, 1).astype(bf16))
        part = mm(slots, back, 0, 0).astype(bf16)
        token_grad.append(lax.psum_scatter(part, "z", scatter_dimension=0, tiled=True))
    token_grad = jnp.concatenate(token_grad, axis=1)
    grad_in = mm(jnp.concatenate(rows_in, axis=1), d_joined, 0, 0)
    grad_out = mm(hidden, jnp.concatenate(rows_grad, axis=1), 0, 0)
    half_width = width // 2
    other = 1 - core

    def sum_cores(x, axis):
        keep = lax.dynamic_slice_in_dim(x, core * half_width, half_width, axis)
        send = lax.dynamic_slice_in_dim(x, other * half_width, half_width, axis)
        got = lax.ppermute(send, "dp", [(0, 1), (1, 0)])
        return (keep + got).astype(bf16)[None]

    return (token_grad, sum_cores(grad_in, 0), sum_cores(grad_out, 1))


def solution(mesh):
    split = Mesh(mesh.devices.reshape(2, Z, X, Y), ("dp", "z", "x", "y"))
    hosts = ("z", "x", "y")
    rows = P(("dp",) + hosts, None)
    in_specs = (rows, rows, rows, rows, P(hosts, None, None), P(hosts, None, None))
    out_specs = (rows, P(hosts, "dp", None), P(hosts, None, "dp"))
    return jax.shard_map(body, mesh=split, in_specs=in_specs, out_specs=out_specs, check_vma=False)
```

profile of v0, /device:TPU:1, one launch (start us, length us, event | category | flops | bytes accessed | tf_op | source)
XLA Modules:
  0.0 320.4 jit_solution(10744743611331638339)
XLA Ops:
  8.0 0.7 all-gather.3.cloned.1.call-update
  8.7 0.7 convert_element_type.42
  9.6 0.7 maximum_bitcast_fusion
  10.3 23.3 %all_gather.9 = f32[64,128]{1,0:T(8,128)S(1)} all-gather(f32[8,128]{1,0:T(8,128)S(1)} %maximum_bitcast_fusion), channel_id=1, replica_groups=mesh['dp'=2,'z'=8,'x'=4,'y'=4] {'z'}, dimensions={0}, use_global_device_ids=true | all-gather | bytes 36864 | tf_op jit(solution)/shard_map/all_gather | solution.py:65
  34.0 0.8 copy-done.3
  34.8 1.5 bitcast_compare_fusion
  36.3 32.3 %all-gather.5.cloned.1.call-done = bf16[1024,2048]{1,0:T(8,128)(2,1)} async-done(((bf16[128,2048]{1,0:T(8,128)(2,1)}), bf16[1024,2048]{1,0:T(8,128)(2,1)}) %all-gather.5.cloned.1.call-update) | async-done | bytes 4194320 | tf_op jit(solution)/shard_map/all_gather | solution.py:65
  68.6 8.2 %convolution_convert_fusion.2 = bf16[896,2048]{1,0:T(8,128)(2,1)} fusion(pred[896,1024]{1,0:T(32,128)(4,1)} %bitcast_compare_fusion, bf16[1024,2048]{1,0:T(8,128)(2,1)} %all-gather.5.cloned.1.call-done), kind=kOutput, calls=%fused_computation.4 | convolution fusion | flops 3759931392 | bytes 8781824 | tf_op jit(solution)/shard_map/dot_general | solution.py:18
  76.8 6.6 %all-to-all-start.1 = ((bf16[16,56,2048]{2,1,0:T(8,128)(2,1)}), bf16[16,56,2048]{2,1,0:T(8,128)(2,1)}, u32[]{:S(2)}, u32[]{:S(2)}) async-start(bf16[16,56,2048]{2,1,0:T(8,128)(2,1)} %bitcast.52), calls=%async_computation.1 | async-start | bytes 7340032 | tf_op jit(solution)/shard_map/all_to_all | solution.py:68
  83.9 39.9 %all-gather.3.cloned.1.call-done = bf16[1024,2048]{1,0:T(8,128)(2,1)} async-done(((bf16[128,2048]{1,0:T(8,128)(2,1)}), bf16[1024,2048]{1,0:T(8,128)(2,1)}) %all-gather.3.cloned.1.call-update) | async-done | bytes 4194320 | tf_op jit(solution)/shard_map/all_gather | solution.py:65
  123.8 8.2 %multiply_convert_fusion = bf16[896,2048]{1,0:T(8,128)(2,1)} fusion(pred[896,1024]{1,0:T(32,128)(4,1)} %bitcast_compare_fusion, bf16[1024,2048]{1,0:T(8,128)(2,1)} %all-gather.3.cloned.1.call-done, f32[896]{0:T(1024)S(1)} %mul.43), kind=kOutput, calls=%fused_computation | convolution fusion | flops 3761766400 | bytes 8785408 | tf_op jit(solution)/shard_map/dot_general | solution.py:18
  132.0 0.8 all-to-all-done.1
  132.8 11.7 %all-to-all-start = ((bf16[16,56,2048]{2,1,0:T(8,128)(2,1)}), bf16[16,56,2048]{2,1,0:T(8,128)(2,1)}, u32[]{:S(2)}, u32[]{:S(2)}) async-start(bf16[16,56,2048]{2,1,0:T(8,128)(2,1)} %bitcast.53), calls=%async_computation | async-start | bytes 7340032 | tf_op jit(solution)/shard_map/all_to_all | solution.py:68
  144.5 7.1 %fusion.1 = f32[896,768]{0,1:T(8,128)} fusion(bf16[896,2048]{1,0:T(8,128)(2,1)} %bitcast.11, bf16[1,2048,768]{2,1,0:T(8,128)(2,1)S(1)} %copy-done), kind=kOutput, calls=%fused_computation.6 | convolution fusion | flops 2818572288 | bytes 9568256 | tf_op jit(solution)/shard_map/dot_general | solution.py:18
  151.6 38.2 %all-to-all-done = bf16[16,56,2048]{2,1,0:T(8,128)(2,1)} async-done(((bf16[16,56,2048]{2,1,0:T(8,128)(2,1)}), bf16[16,56,2048]{2,1,0:T(8,128)(2,1)}, u32[]{:S(2)}, u32[]{:S(2)}) %all-to-all-start) | async-done | bytes 3670048 | tf_op jit(solution)/shard_map/all_to_all | solution.py:68
  189.8 5.4 %multiply_convert_fusion.3 = (bf16[896,384]{0,1:T(8,128)(2,1)S(1)}, bf16[896,384]{0,1:T(8,128)(2,1)S(1)}) fusion(f32[896,768]{0,1:T(8,128)} %fusion.1, bf16[896,2048]{1,0:T(8,128)(2,1)} %bitcast.8, bf16[1,384,2048]{2,1,0:T(8,128)(2,1)} %param.11), kind=kOutput, calls=%fused_computation.17 | convolution fusion | flops 1413758976 | bytes 9371648 | tf_op jit(solution)/shard_map/dot_general | solution.py:18
  195.2 4.6 %convolution_convert_fusion.1 = bf16[896,2048]{1,0:T(8,128)(2,1)} fusion(bf16[1,2048,768]{2,1,0:T(8,128)(2,1)S(1)} %copy-done, bf16[896,384]{0,1:T(8,128)(2,1)S(1)} %get-tuple-element.4, bf16[896,384]{0,1:T(8,128)(2,1)S(1)} %get-tuple-element.3), kind=kOutput, calls=%fused_computation.3 | convolution fusion | flops 2823159808 | bytes 8192000 | tf_op jit(solution)/shard_map/dot_general | solution.py:18
  199.8 4.6 %all-to-all-start.2 = ((bf16[16,56,2048]{2,1,0:T(8,128)(2,1)}), bf16[16,56,2048]{2,1,0:T(8,128)(2,1)}, u32[]{:S(2)}, u32[]{:S(2)}) async-start(bf16[16,56,2048]{2,1,0:T(8,128)(2,1)} %bitcast.54), calls=%async_computation.2 | async-start | bytes 7340032 | tf_op jit(solution)/shard_map/all_to_all | solution.py:68
  205.3 42.5 %all-to-all-done.2 = bf16[16,56,2048]{2,1,0:T(8,128)(2,1)} async-done(((bf16[16,56,2048]{2,1,0:T(8,128)(2,1)}), bf16[16,56,2048]{2,1,0:T(8,128)(2,1)}, u32[]{:S(2)}, u32[]{:S(2)}) %all-to-all-start.2) | async-done | bytes 3670048 | tf_op jit(solution)/shard_map/all_to_all | solution.py:68
  247.8 8.2 %convolution_convert_fusion = bf16[1024,2048]{1,0:T(8,128)(2,1)} fusion(pred[896,1024]{1,0:T(8,128)(4,1)S(1)} %bitcast.55, bf16[896,2048]{1,0:T(8,128)(2,1)} %bitcast.14), kind=kOutput, calls=%fused_computation.1 | convolution fusion | flops 3760193536 | bytes 8781824 | tf_op jit(solution)/shard_map/dot_general | solution.py:18
  256.1 1.1 copy-done.8
  257.3 5.6 %fusion.7 = f32[2048,768]{1,0:T(8,128)S(1)} fusion(bf16[896,2048]{1,0:T(8,128)(2,1)} %bitcast.11, bf16[896,384]{0,1:T(8,128)(2,1)S(1)} %copy-done.10, bf16[896,384]{0,1:T(8,128)(2,1)S(1)} %copy-done.8), kind=kOutput, calls=%fused_computation.21 | convolution fusion | flops 2821324800 | bytes 11337728 | tf_op jit(solution)/shard_map/dot_general | solution.py:18
  263.0 1.8 constant_dynamic-slice_fusion.1
  264.8 2.2 copy-done.2
  267.0 4.7 %collective-permute-start = (f32[1024,768]{1,0:T(8,128)}, f32[1024,768]{1,0:T(8,128)}, u32[]{:S(2)}, u32[]{:S(2)}) collective-permute-start(f32[1024,768]{1,0:T(8,128)} %constant_dynamic-slice_fusion.1), channel_id=1, source_target_pairs={{0,128},{128,0},{1,129},{129,1},{2,130},{130,2},{3,131},{131,3},{4... | collective-permute-start | bytes 9437192 | tf_op jit(solution)/shard_map/ppermute | solution.py:106
  271.7 3.9 %fusion.9 = f32[384,2048]{1,0:T(8,128)S(1)} fusion(bf16[896,2048]{1,0:T(8,128)(2,1)} %bitcast.8, f32[896,768]{0,1:T(8,128)S(1)} %copy-done.6), kind=kOutput, calls=%fused_computation.23 | convolution fusion | flops 1411350528 | bytes 9568256 | tf_op jit(solution)/shard_map/dot_general | solution.py:18
  275.6 1.8 copy-done.5
  277.4 1.3 constant_dynamic-slice_fusion
  278.7 3.7 %collective-permute-done.1 = f32[384,1024]{1,0:T(8,128)} collective-permute-done((f32[384,1024]{1,0:T(8,128)}, f32[384,1024]{1,0:T(8,128)}, u32[]{:S(2)}, u32[]{:S(2)}) %collective-permute-start.1) | collective-permute-done | bytes 1572896 | tf_op jit(solution)/shard_map/ppermute | solution.py:106
  282.4 3.2 fusion.8
  285.6 4.4 %fusion.3 = bf16[1,1024,768]{2,1,0:T(8,128)(2,1)} fusion(f32[1024,768]{1,0:T(8,128)} %collective-permute-done, f32[2048,768]{1,0:T(8,128)} %copy-done.2, s32[]{:T(128)S(6)} %select_n.37), kind=kLoop, calls=%fused_computation.10 | loop fusion | flops 1572864 | bytes 7864324 | tf_op jit(solution)/shard_map/broadcast_in_dim | solution.py:107
  290.0 23.9 %reduce-scatter.2.cloned.1.call-done = bf16[128,2048]{1,0:T(8,128)(2,1)} async-done(((bf16[1024,2048]{1,0:T(8,128)(2,1)}), bf16[128,2048]{1,0:T(8,128)(2,1)}) %reduce-scatter.2.cloned.1.call-update) | async-done | bytes 524304 | tf_op jit(solution)/shard_map/reduce_scatter | solution.py:96
  (43 shorter events, 3.0 us)
Async XLA Ops:
  7.2 137.4 %copy-start = (bf16[1,2048,768]{2,1,0:T(8,128)(2,1)S(1)}, bf16[1,2048,768]{2,1,0:T(8,128)(2,1)}, u32[]{:S(2)}) copy-start(bf16[1,2048,768]{2,1,0:T(8,128)(2,1)} %param.10) | copy-start | bytes 9437188
  7.2 61.4 %all-gather.5.cloned.1.call-start = ((), (), s32[]{:S(2)}) async-start(), calls=%async_computation.5 | async-start | bytes 4718592 | tf_op jit(solution)/shard_map/all_gather | solution.py:65
  7.9 115.9 %all-gather.3.cloned.1.call-start = ((), (), s32[]{:S(2)}) async-start(), calls=%async_computation.4 | async-start | bytes 4718592 | tf_op jit(solution)/shard_map/all_gather | solution.py:65
  34.0 0.8 copy-start.3
  76.8 56.0 %all-to-all-start.1 = ((bf16[16,56,2048]{2,1,0:T(8,128)(2,1)}), bf16[16,56,2048]{2,1,0:T(8,128)(2,1)}, u32[]{:S(2)}, u32[]{:S(2)}) async-start(bf16[16,56,2048]{2,1,0:T(8,128)(2,1)} %bitcast.52), calls=%async_computation.1 | async-start | bytes 7340032 | tf_op jit(solution)/shard_map/all_to_all | solution.py:68
  132.8 57.0 %all-to-all-start = ((bf16[16,56,2048]{2,1,0:T(8,128)(2,1)}), bf16[16,56,2048]{2,1,0:T(8,128)(2,1)}, u32[]{:S(2)}, u32[]{:S(2)}) async-start(bf16[16,56,2048]{2,1,0:T(8,128)(2,1)} %bitcast.53), calls=%async_computation | async-start | bytes 7340032 | tf_op jit(solution)/shard_map/all_to_all | solution.py:68
  195.2 4.6 %copy-start.7 = (bf16[896,384]{0,1:T(8,128)(2,1)}, bf16[896,384]{0,1:T(8,128)(2,1)S(1)}, u32[]{:S(2)}) copy-start(bf16[896,384]{0,1:T(8,128)(2,1)S(1)} %get-tuple-element.3) | copy-start | bytes 2064388
  195.2 4.6 %copy-start.9 = (bf16[896,384]{0,1:T(8,128)(2,1)}, bf16[896,384]{0,1:T(8,128)(2,1)S(1)}, u32[]{:S(2)}) copy-start(bf16[896,384]{0,1:T(8,128)(2,1)S(1)} %get-tuple-element.4) | copy-start | bytes 2064388
  199.8 4.9 %copy-start.4 = (f32[16,8,1024]{2,1,0:T(8,128)S(1)}, f32[16,8,1024]{2,1,0:T(8,128)}, u32[]{:S(2)}) copy-start(f32[16,8,1024]{2,1,0:T(8,128)} %copy-done.3) | copy-start | bytes 1572868
  199.8 48.0 %all-to-all-start.2 = ((bf16[16,56,2048]{2,1,0:T(8,128)(2,1)}), bf16[16,56,2048]{2,1,0:T(8,128)(2,1)}, u32[]{:S(2)}, u32[]{:S(2)}) async-start(bf16[16,56,2048]{2,1,0:T(8,128)(2,1)} %bitcast.54), calls=%async_computation.2 | async-start | bytes 7340032 | tf_op jit(solution)/shard_map/all_to_all | solution.py:68
  204.5 109.4 %reduce-scatter.2.cloned.1.call-start = ((), (), s32[]{:S(2)}) async-start(), calls=%async_computation.6 | async-start | bytes 4718592 | tf_op jit(solution)/shard_map/reduce_scatter | solution.py:96
  256.0 1.1 copy-start.8
  256.0 1.3 copy-start.10
  262.9 4.0 %copy-start.2 = (f32[2048,768]{1,0:T(8,128)}, f32[2048,768]{1,0:T(8,128)S(1)}, u32[]{:S(2)}) copy-start(f32[2048,768]{1,0:T(8,128)S(1)} %fusion.7) | copy-start | bytes 18874372
  263.0 8.7 %copy-start.6 = (f32[896,768]{0,1:T(8,128)S(1)}, f32[896,768]{0,1:T(8,128)}, u32[]{:S(2)}) copy-start(f32[896,768]{0,1:T(8,128)} %fusion.1) | copy-start | bytes 8257540
  267.0 18.6 %collective-permute-start = (f32[1024,768]{1,0:T(8,128)}, f32[1024,768]{1,0:T(8,128)}, u32[]{:S(2)}, u32[]{:S(2)}) collective-permute-start(f32[1024,768]{1,0:T(8,128)} %constant_dynamic-slice_fusion.1), channel_id=1, source_target_pairs={{0,128},{128,0},{1,129},{129,1},{2,130},{130,2},{3,131},{131,3},{4... | collective-permute-start | bytes 9437192 | tf_op jit(solution)/shard_map/ppermute | solution.py:106
  275.6 1.8 copy-start.5
  278.7 3.8 %collective-permute-start.1 = (f32[384,1024]{1,0:T(8,128)}, f32[384,1024]{1,0:T(8,128)}, u32[]{:S(2)}, u32[]{:S(2)}) collective-permute-start(f32[384,1024]{1,0:T(8,128)} %constant_dynamic-slice_fusion), channel_id=1, source_target_pairs={{0,128},{128,0},{1,129},{129,1},{2,130},{130,2},{3,131},{131,3},{4... | collective-permute-start | bytes 4718600 | tf_op jit(solution)/shard_map/ppermute | solution.py:106
  282.4 31.4 %copy-start.1 = (bf16[1,2048,768]{2,1,0:T(8,128)(2,1)S(1)}, bf16[1,2048,768]{2,1,0:T(8,128)(2,1)}, u32[]{:S(2)}) copy-start(bf16[1,2048,768]{2,1,0:T(8,128)(2,1)} %param.10) | copy-start | bytes 9437188
Sparse Core Ops, SparseCore 0:
  9.8 58.7 all-gather.4
  70.4 53.4 all-gather.2
  256.2 57.6 reduce-scatter.1
where the time goes:
time: 321 us; the launch traced here: 320 us
  waiting for transfers between devices  183 us (57%)
  matrix products  51.4 us (16%)
  starting transfers between devices  28 us (9%)
  blocking collectives  23.3 us (7%)
  between operations  14 us (4%)
  other arithmetic  11.5 us (4%)
  local copies, waits for them, and re-layouts  9.6 us (3%)
    all_to_all x3, waiting for transfers between devices, swap_plane(): lax.all_to_all(x, ('x', 'y'), split_axis=0, concat_axis=0, tiled=True)  81.4 us
    all_gather x2, waiting for transfers between devices, gather_z(): return lax.all_gather(x, 'z', axis=0, tiled=True)  72.2 us
    dot_general x9, matrix products, mm(): lax.dot_general(a, b, (((ca,), (cb,)), ((), ())), preferred_element_type=...  51.4 us
    reduce_scatter x1, waiting for transfers between devices, body(): lax.psum_scatter(part, 'z', scatter_dimension=0, tiled=True)  23.9 us
    all_gather x1, blocking collectives, gather_z(): return lax.all_gather(x, 'z', axis=0, tiled=True)  23.3 us
    all_to_all x3, starting transfers between devices, swap_plane(): lax.all_to_all(x, ('x', 'y'), split_axis=0, concat_axis=0, tiled=True)  23 us
    broadcast_in_dim x2, other arithmetic, sum_cores(): return (keep + got).astype(bf16)[None]  7.52 us
  transfers between devices with their start and end apart: 8, of which 7 were waited for; matrix products, arithmetic and copies ran while one was open for 15% of the time, Pallas kernels for 0%

commit v1 on v0

--- a/solution.py
+++ b/solution.py
@@ -12,6 +12,11 @@
 BACK_CHUNKS = 1
 f32 = jnp.float32
 bf16 = jnp.bfloat16
+
+
+def exchange_gather(x, axis, d):
+    stack = jnp.stack([x] * lax.axis_size(axis))
+    return jnp.concatenate(lax.all_to_all(stack, axis, 0, 0), axis=d)
 
 
 def mm(a, b, ca, cb):
@@ -62,7 +67,7 @@
     core = lax.axis_index("dp")
 
     def gather_z(x):
-        return lax.all_gather(x, "z", axis=0, tiled=True)
+        return exchange_gather(x, "z", 0)
 
     def swap_plane(x):
         return lax.all_to_all(x, ("x", "y"), split_axis=0, concat_axis=0, tiled=True)

time: 321 us -> 451 us (1.40)
  blocking collectives: 23.3 us -> 165 us
  waiting for transfers between devices: 183 us -> 173 us
    all_to_all x0 -> x3, blocking collectives: none -> 165 us  [the longest x2 112 us: exchange_gather(): return jnp.concatenate(lax.all_to_all(stack, axis, 0, 0), axis=d)]
    all_to_all x0 -> x1, waiting for transfers between devices: none -> 81.6 us  [exchange_gather(): return jnp.concatenate(lax.all_to_all(stack, axis, 0, 0), axis=d)]
    all_gather x2 -> x0, waiting for transfers between devices: 72.2 us -> none  [gather_z(): return lax.all_gather(x, 'z', axis=0, tiled=True)]
    all_gather x1 -> x0, blocking collectives: 23.3 us -> none  [gather_z(): return lax.all_gather(x, 'z', axis=0, tiled=True)]
    all_to_all x3 -> x2, waiting for transfers between devices: 81.4 us -> 62.3 us  [swap_plane(): lax.all_to_all(x, ('x', 'y'), split_axis=0, concat_axis=0, tiled=True)]
    all_to_all x3 -> x2, starting transfers between devices: 23 us -> 16.3 us  [swap_plane(): lax.all_to_all(x, ('x', 'y'), split_axis=0, concat_axis=0, tiled=True)]
    all_to_all x0 -> x1, starting transfers between devices: none -> 4.55 us  [exchange_gather(): return jnp.concatenate(lax.all_to_all(stack, axis, 0, 0), axis=d)]
  transfers between devices with their start and end apart: 8 -> 6, of which waited for: 7 -> 5; matrix products, arithmetic and copies ran while one was open for 15% -> 10% of each run, Pallas kernels for 0% -> 0%
where the time goes in v1:
time: 451 us; the launch traced here: 450 us
  waiting for transfers between devices  173 us (38%)
  blocking collectives  165 us (37%)
  matrix products  47.5 us (11%)
  starting transfers between devices  27.4 us (6%)
  between operations  14.3 us (3%)
  local copies, waits for them, and re-layouts  13.6 us (3%)
  other arithmetic  10.3 us (2%)
    all_to_all x2, blocking collectives, exchange_gather(): return jnp.concatenate(lax.all_to_all(stack, axis, 0, 0), axis=d)  112 us
    all_to_all x1, waiting for transfers between devices, exchange_gather(): return jnp.concatenate(lax.all_to_all(stack, axis, 0, 0), axis=d)  81.6 us
    all_to_all x2, waiting for transfers between devices, swap_plane(): lax.all_to_all(x, ('x', 'y'), split_axis=0, concat_axis=0, tiled=True)  62.3 us
    all_to_all x1, blocking collectives, swap_plane(): lax.all_to_all(x, ('x', 'y'), split_axis=0, concat_axis=0, tiled=True)  52.3 us
    dot_general x9, matrix products, mm(): lax.dot_general(a, b, (((ca,), (cb,)), ((), ())), preferred_element_type=...  47.5 us
    reduce_scatter x1, waiting for transfers between devices, body(): lax.psum_scatter(part, 'z', scatter_dimension=0, tiled=True)  25.2 us
    all_to_all x2, starting transfers between devices, swap_plane(): lax.all_to_all(x, ('x', 'y'), split_axis=0, concat_axis=0, tiled=True)  16.3 us
  transfers between devices with their start and end apart: 6, of which 5 were waited for; matrix products, arithmetic and copies ran while one was open for 10% of the time, Pallas kernels for 0%

profile of v1, /device:TPU:1, one launch (start us, length us, event | category | flops | bytes accessed | tf_op | source)
XLA Modules:
  0.0 450.4 jit_solution(3490570285598767060)
XLA Ops:
  7.2 0.8 convert_element_type.40
  8.0 0.8 maximum_bitcast_fusion
  8.8 15.7 %all_to_all.51 = f32[8,8,128]{2,1,0:T(8,128)S(1)} all-to-all(f32[8,8,128]{2,1,0:T(8,128)S(1)} %stack.6), channel_id=1, replica_groups=mesh['dp'=2,'z'=8,'x'=4,'y'=4] {'z'}, dimensions={0} | all-to-all | bytes 65536 | tf_op jit(solution)/shard_map/all_to_all | solution.py:19
  24.5 1.6 stack.8
  26.1 96.6 %all_to_all.52 = bf16[8,128,2048]{2,1,0:T(8,128)(2,1)} all-to-all(bf16[8,128,2048]{2,1,0:T(8,128)(2,1)S(1)} %stack.8), channel_id=1, replica_groups=mesh['dp'=2,'z'=8,'x'=4,'y'=4] {'z'}, dimensions={0} | all-to-all | bytes 8388608 | tf_op jit(solution)/shard_map/all_to_all | solution.py:19
  122.7 2.5 stack.7
  125.2 4.6 %all-to-all-start.1 = ((bf16[8,128,2048]{2,1,0:T(8,128)(2,1)}), bf16[8,128,2048]{2,1,0:T(8,128)(2,1)}, u32[]{:S(2)}, u32[]{:S(2)}) async-start(bf16[8,128,2048]{2,1,0:T(8,128)(2,1)} %stack.7), calls=%async_computation.1 | async-start | bytes 8388608 | tf_op jit(solution)/shard_map/all_to_all | solution.py:19
  130.8 0.9 copy-done.4
  131.7 7.6 %convolution_convert_fusion.2 = bf16[896,2048]{1,0:T(8,128)(2,1)} fusion(pred[896,1024]{1,0:T(8,128)(4,1)S(1)} %bitcast.56, bf16[1024,2048]{1,0:T(8,128)(2,1)} %bitcast.51), kind=kOutput, calls=%fused_computation.3 | convolution fusion | flops 3759931392 | bytes 8781824 | tf_op jit(solution)/shard_map/dot_general | solution.py:23
  139.3 81.6 %all-to-all-done.1 = bf16[8,128,2048]{2,1,0:T(8,128)(2,1)} async-done(((bf16[8,128,2048]{2,1,0:T(8,128)(2,1)}), bf16[8,128,2048]{2,1,0:T(8,128)(2,1)}, u32[]{:S(2)}, u32[]{:S(2)}) %all-to-all-start.1) | async-done | bytes 4194336 | tf_op jit(solution)/shard_map/all_to_all | solution.py:19
  220.9 6.8 %all-to-all-start.4 = ((bf16[16,56,2048]{2,1,0:T(8,128)(2,1)}), bf16[16,56,2048]{2,1,0:T(8,128)(2,1)}, u32[]{:S(2)}, u32[]{:S(2)}) async-start(bf16[16,56,2048]{2,1,0:T(8,128)(2,1)} %bitcast.52), calls=%async_computation.4 | async-start | bytes 7340032 | tf_op jit(solution)/shard_map/all_to_all | solution.py:73
  228.2 8.2 %multiply_convert_fusion = bf16[896,2048]{1,0:T(8,128)(2,1)} fusion(pred[896,1024]{1,0:T(8,128)(4,1)} %bitcast.57, bf16[1024,2048]{1,0:T(8,128)(2,1)} %bitcast.4, f32[896]{0:T(1024)S(1)} %mul.43), kind=kOutput, calls=%fused_computation | convolution fusion | flops 3761766400 | bytes 8785408 | tf_op jit(solution)/shard_map/dot_general | solution.py:23
  236.4 31.8 %all-to-all-done.4 = bf16[16,56,2048]{2,1,0:T(8,128)(2,1)} async-done(((bf16[16,56,2048]{2,1,0:T(8,128)(2,1)}), bf16[16,56,2048]{2,1,0:T(8,128)(2,1)}, u32[]{:S(2)}, u32[]{:S(2)}) %all-to-all-start.4) | async-done | bytes 3670048 | tf_op jit(solution)/shard_map/all_to_all | solution.py:73
  268.2 9.5 %all-to-all-start.2 = ((bf16[16,56,2048]{2,1,0:T(8,128)(2,1)}), bf16[16,56,2048]{2,1,0:T(8,128)(2,1)}, u32[]{:S(2)}, u32[]{:S(2)}) async-start(bf16[16,56,2048]{2,1,0:T(8,128)(2,1)} %bitcast.53), calls=%async_computation.2 | async-start | bytes 7340032 | tf_op jit(solution)/shard_map/all_to_all | solution.py:73
  277.9 7.0 %fusion.1 = f32[896,768]{0,1:T(8,128)} fusion(bf16[896,2048]{1,0:T(8,128)(2,1)} %bitcast.11, bf16[1,2048,768]{2,1,0:T(8,128)(2,1)S(1)} %copy-done), kind=kOutput, calls=%fused_computation.5 | convolution fusion | flops 2818572288 | bytes 9568256 | tf_op jit(solution)/shard_map/dot_general | solution.py:23
  285.0 30.5 %all-to-all-done.2 = bf16[16,56,2048]{2,1,0:T(8,128)(2,1)} async-done(((bf16[16,56,2048]{2,1,0:T(8,128)(2,1)}), bf16[16,56,2048]{2,1,0:T(8,128)(2,1)}, u32[]{:S(2)}, u32[]{:S(2)}) %all-to-all-start.2) | async-done | bytes 3670048 | tf_op jit(solution)/shard_map/all_to_all | solution.py:73
  315.5 5.4 %multiply_convert_fusion.3 = (bf16[896,384]{0,1:T(8,128)(2,1)S(1)}, bf16[896,384]{0,1:T(8,128)(2,1)S(1)}) fusion(f32[896,768]{0,1:T(8,128)} %fusion.1, bf16[896,2048]{1,0:T(8,128)(2,1)} %bitcast.7, bf16[1,384,2048]{2,1,0:T(8,128)(2,1)} %param.11), kind=kOutput, calls=%fused_computation.16 | convolution fusion | flops 1413758976 | bytes 9371648 | tf_op jit(solution)/shard_map/dot_general | solution.py:23
  320.9 3.3 convolution_convert_fusion.1
  324.3 52.3 %all_to_all.53 = bf16[16,56,2048]{2,1,0:T(8,128)(2,1)S(1)} all-to-all(bf16[16,56,2048]{2,1,0:T(8,128)(2,1)S(1)} %bitcast.55), channel_id=1, replica_groups=mesh['dp'=2,'z'=8,'x'=4,'y'=4] {'x','y'}, dimensions={0} | all-to-all | bytes 7340032 | tf_op jit(solution)/shard_map/all_to_all | solution.py:73
  376.6 6.3 %convolution_convert_fusion = bf16[1024,2048]{1,0:T(8,128)(2,1)} fusion(pred[896,1024]{1,0:T(8,128)(4,1)S(1)} %bitcast.58, bf16[896,2048]{1,0:T(8,128)(2,1)S(1)} %bitcast.54), kind=kOutput, calls=%fused_computation.1 | convolution fusion | flops 3760193536 | bytes 8781824 | tf_op jit(solution)/shard_map/dot_general | solution.py:23
  382.9 1.1 copy-done.9
  384.2 5.6 %fusion.7 = f32[2048,768]{1,0:T(8,128)S(1)} fusion(bf16[896,2048]{1,0:T(8,128)(2,1)} %bitcast.11, bf16[896,384]{0,1:T(8,128)(2,1)S(1)} %copy-done.11, bf16[896,384]{0,1:T(8,128)(2,1)S(1)} %copy-done.9), kind=kOutput, calls=%fused_computation.20 | convolution fusion | flops 2821324800 | bytes 11337728 | tf_op jit(solution)/shard_map/dot_general | solution.py:23
  389.8 1.9 constant_dynamic-slice_fusion.1
  391.7 2.1 copy-done.2
  393.9 6.2 %collective-permute-start = (f32[1024,768]{1,0:T(8,128)}, f32[1024,768]{1,0:T(8,128)}, u32[]{:S(2)}, u32[]{:S(2)}) collective-permute-start(f32[1024,768]{1,0:T(8,128)} %constant_dynamic-slice_fusion.1), channel_id=1, source_target_pairs={{0,128},{128,0},{1,129},{129,1},{2,130},{130,2},{3,131},{131,3},{4... | collective-permute-start | bytes 9437192 | tf_op jit(solution)/shard_map/ppermute | solution.py:111
  400.1 3.9 fusion.9
  404.0 1.8 copy-done.3
  405.8 1.3 constant_dynamic-slice_fusion
  407.3 3.6 collective-permute-done.1
  410.9 3.2 fusion.8
  414.0 4.3 fusion.3
  418.4 25.2 %reduce-scatter.2.cloned.1.call-done = bf16[128,2048]{1,0:T(8,128)(2,1)} async-done(((bf16[1024,2048]{1,0:T(8,128)(2,1)}), bf16[128,2048]{1,0:T(8,128)(2,1)}) %reduce-scatter.2.cloned.1.call-update) | async-done | bytes 524304 | tf_op jit(solution)/shard_map/reduce_scatter | solution.py:101
  (41 shorter events, 2.2 us)
Async XLA Ops:
  7.2 270.8 %copy-start = (bf16[1,2048,768]{2,1,0:T(8,128)(2,1)S(1)}, bf16[1,2048,768]{2,1,0:T(8,128)(2,1)}, u32[]{:S(2)}) copy-start(bf16[1,2048,768]{2,1,0:T(8,128)(2,1)} %param.10) | copy-start | bytes 9437188
  26.1 96.6 %copy-start.6 = (bf16[128,2048]{1,0:T(8,128)(2,1)S(1)}, bf16[128,2048]{1,0:T(8,128)(2,1)}, u32[]{:S(2)}) copy-start(bf16[128,2048]{1,0:T(8,128)(2,1)} %param.7) | copy-start | bytes 1572868
  125.2 95.7 %all-to-all-start.1 = ((bf16[8,128,2048]{2,1,0:T(8,128)(2,1)}), bf16[8,128,2048]{2,1,0:T(8,128)(2,1)}, u32[]{:S(2)}, u32[]{:S(2)}) async-start(bf16[8,128,2048]{2,1,0:T(8,128)(2,1)} %stack.7), calls=%async_computation.1 | async-start | bytes 8388608 | tf_op jit(solution)/shard_map/all_to_all | solution.py:19
  130.8 0.9 copy-start.4
  220.9 47.3 %all-to-all-start.4 = ((bf16[16,56,2048]{2,1,0:T(8,128)(2,1)}), bf16[16,56,2048]{2,1,0:T(8,128)(2,1)}, u32[]{:S(2)}, u32[]{:S(2)}) async-start(bf16[16,56,2048]{2,1,0:T(8,128)(2,1)} %bitcast.52), calls=%async_computation.4 | async-start | bytes 7340032 | tf_op jit(solution)/shard_map/all_to_all | solution.py:73
  268.2 47.3 %all-to-all-start.2 = ((bf16[16,56,2048]{2,1,0:T(8,128)(2,1)}), bf16[16,56,2048]{2,1,0:T(8,128)(2,1)}, u32[]{:S(2)}, u32[]{:S(2)}) async-start(bf16[16,56,2048]{2,1,0:T(8,128)(2,1)} %bitcast.53), calls=%async_computation.2 | async-start | bytes 7340032 | tf_op jit(solution)/shard_map/all_to_all | solution.py:73
  277.7 165.8 %reduce-scatter.2.cloned.1.call-start = ((), (), s32[]{:S(2)}) async-start(), calls=%async_computation.7 | async-start | bytes 4718592 | tf_op jit(solution)/shard_map/reduce_scatter | solution.py:101
  320.9 3.4 copy-start.8
  320.9 3.4 copy-start.10
  324.3 52.3 %copy-start.5 = (pred[16,7,8,1024]{3,2,1,0:T(8,128)(4,1)S(1)}, pred[16,7,8,1024]{3,2,1,0:T(8,128)(4,1)}, u32[]{:S(2)}) copy-start(pred[16,7,8,1024]{3,2,1,0:T(8,128)(4,1)} %copy-done.4) | copy-start | bytes 2752516
  382.9 1.1 copy-start.9
  382.9 1.3 copy-start.11
  389.8 4.0 copy-start.2
  389.8 10.2 %copy-start.7 = (f32[896,768]{0,1:T(8,128)S(1)}, f32[896,768]{0,1:T(8,128)}, u32[]{:S(2)}) copy-start(f32[896,768]{0,1:T(8,128)} %fusion.1) | copy-start | bytes 8257540
  393.9 20.1 %collective-permute-start = (f32[1024,768]{1,0:T(8,128)}, f32[1024,768]{1,0:T(8,128)}, u32[]{:S(2)}, u32[]{:S(2)}) collective-permute-start(f32[1024,768]{1,0:T(8,128)} %constant_dynamic-slice_fusion.1), channel_id=1, source_target_pairs={{0,128},{128,0},{1,129},{129,1},{2,130},{130,2},{3,131},{131,3},{4... | collective-permute-start | bytes 9437192 | tf_op jit(solution)/shard_map/ppermute | solution.py:111
  404.0 1.8 copy-start.3
  407.1 3.8 collective-permute-start.1
  410.8 32.7 %copy-start.1 = (bf16[1,2048,768]{2,1,0:T(8,128)(2,1)S(1)}, bf16[1,2048,768]{2,1,0:T(8,128)(2,1)}, u32[]{:S(2)}) copy-start(bf16[1,2048,768]{2,1,0:T(8,128)(2,1)} %param.10) | copy-start | bytes 9437188
Sparse Core Ops, SparseCore 0:
  383.1 60.4 reduce-scatter.1
